TPU v7x, 256 devices: a whole 4x4x8 slice. The times are simulated.
256 devices in a mesh: seq: 32 (over z, x), tp: 8 (over y, core).
Axes of the slice: x: 4, y: 4, z: 8, core: 2. Of those that a mesh axis runs over, the one named last changes fastest.
Arguments:
- tokens_in: bfloat16 [8, 4, 2560], P(None, None, 'tp'), may hold values from -32 to 32
- attn_gain: bfloat16 [2560], replicated, may hold values from 0.25 to 1.75
- mlp_gain: bfloat16 [2560], replicated, may hold values from 0.25 to 1.75
- proj_query: bfloat16 [2560, 2560], P(None, 'tp'), may hold values from -0.125 to 0.125
- proj_key: bfloat16 [2560, 640], P(None, 'tp'), may hold values from -0.125 to 0.125
- proj_value: bfloat16 [2560, 640], P(None, 'tp'), may hold values from -0.125 to 0.125
- proj_out: bfloat16 [2560, 2560], P('tp'), may hold values from -0.125 to 0.125
- proj_gate: bfloat16 [2560, 3456], P(None, 'tp'), may hold values from -0.125 to 0.125
- proj_up: bfloat16 [2560, 3456], P(None, 'tp'), may hold values from -0.125 to 0.125
- proj_down: bfloat16 [3456, 2560], P('tp'), may hold values from -0.109375 to 0.109375
- long_keys: bfloat16 [4096, 8, 80], P('seq', 'tp'), may hold values from -340 to 340
- long_values: bfloat16 [4096, 8, 80], P('seq', 'tp'), may hold values from -6 to 6
- short_keys: bfloat16 [512, 8, 240], P('seq', 'tp'), may hold values from -340 to 340
- short_values: bfloat16 [512, 8, 240], P('seq', 'tp'), may hold values from -6 to 6
- long_seen: int32 [1], replicated, may hold values from 4096 to 8191
- short_len: int32 [3], replicated, may hold values from 1 to 504, as said below
Outputs:
- layer_out: bfloat16 [8, 4, 2560], P(None, None, 'tp')
Inputs may be any that keep to these rules, and one draw needn't show every extreme that they name: `short_len`: some short request has exactly 504 cached tokens and some exactly 1.
All inputs are finite; a program needn't handle non-finite values.
Results may differ from a plain program's by a relative error of at most 0.01.
Values may be sent and summed in bfloat16 or wider, within the bound.
No kernel may reach another device: no remote copies, remote signals or barrier semaphores. Data moves between devices by JAX's collectives and lax.ppermute only.
A program may use at most 128 MiB of HBM per device.

v0:
```python
import math
import jax
import jax.numpy as jnp
from jax import lax
from jax.sharding import PartitionSpec as P

HEADS = 32
KV_HEADS = 8
HD = 80
WIN = 4096
STEPS = 8
LONG = 1
eps_norm = 1e-05
theta_base = 10000.0
masked_score = -1e30


def rms_scaled(hidden_rows, norm_gain):
    mean_square = jnp.mean(hidden_rows * hidden_rows, axis=-1, keepdims=True)
    return hidden_rows * lax.rsqrt(mean_square + eps_norm) * norm_gain.astype(jnp.float32)


def rotate(vectors, positions):
    half_width = vectors.shape[-1] // 2
    freq_index = jnp.arange(half_width, dtype=jnp.float32)
    frequency = theta_base ** (-2.0 * freq_index / vectors.shape[-1])
    angles = positions.astype(jnp.float32)[..., None] * frequency
    view_shape = angles.shape[:2] + (1,) * (vectors.ndim - 3) + (half_width,)
    cosine_table = jnp.cos(angles).reshape(view_shape)
    sine_table = jnp.sin(angles).reshape(view_shape)
    front_part = vectors[..., :half_width]
    back_part = vectors[..., half_width:]
    return jnp.concatenate(
        [
            front_part * cosine_table - back_part * sine_table,
            back_part * cosine_table + front_part * sine_table,
        ],
        axis=-1,
    )


def partial_softmax(queries, cache_keys, cache_values, valid_mask):
    score_scale = 1.0 / math.sqrt(queries.shape[-1])
    scores = (
        jnp.einsum("trkgd,wkrd->trkgw", queries, cache_keys, preferred_element_type=jnp.float32)
        * score_scale
    )
    live_mask = valid_mask[:, :, None, None, :]
    scores = jnp.where(live_mask, scores, masked_score)
    top_score = jnp.max(scores, axis=-1)
    weights = jnp.where(live_mask, jnp.exp(scores - top_score[..., None]), 0.0)
    weight_sum = jnp.sum(weights, axis=-1)
    weighted = jnp.einsum(
        "trkgw,wkrd->trkgd",
        weights.astype(jnp.bfloat16),
        cache_values,
        preferred_element_type=jnp.float32,
    )
    return (top_score, weight_sum, weighted)


def body(
    tokens_in,
    attn_gain,
    mlp_gain,
    proj_query,
    proj_key,
    proj_value,
    proj_out,
    proj_gate,
    proj_up,
    proj_down,
    long_keys,
    long_values,
    short_keys,
    short_values,
    long_seen,
    short_len,
):
    seq_rank = lax.axis_index("seq")
    tp_rank = lax.axis_index("tp")
    local_width = tokens_in.shape[2]
    model_width = proj_query.shape[0]
    total_reqs = tokens_in.shape[1]
    group_size = HEADS // KV_HEADS
    kv_local = proj_key.shape[1] // HD
    base_pos = jnp.concatenate([long_seen, short_len])
    roll_start = long_seen % WIN
    long_slots = long_keys.shape[0]
    short_slots = short_keys.shape[0]
    long_global = seq_rank * long_slots + jnp.arange(long_slots, dtype=jnp.int32)
    long_age = (long_global[None, :] - roll_start[:, None]) % WIN
    short_global = seq_rank * short_slots + jnp.arange(short_slots, dtype=jnp.int32)
    short_live = short_global[None, :] < short_len[:, None]
    long_key_view = long_keys.reshape(long_slots, kv_local, LONG, HD)
    long_value_view = long_values.reshape(long_slots, kv_local, LONG, HD)
    short_key_view = short_keys.reshape(short_slots, kv_local, total_reqs - LONG, HD)
    short_value_view = short_values.reshape(short_slots, kv_local, total_reqs - LONG, HD)
    collected = []
    prior_keys = []
    prior_values = []
    for step_num in range(STEPS):
        token_rows = tokens_in[step_num : step_num + 1]
        block_steps = token_rows.shape[0]
        full_rows = lax.all_gather(token_rows, "tp", axis=2, tiled=True)
        normed = rms_scaled(full_rows.astype(jnp.float32), attn_gain).astype(jnp.bfloat16)
        flat_rows = normed.reshape(block_steps * total_reqs, model_width)
        steps_here = step_num + jnp.arange(block_steps, dtype=jnp.int32)
        positions = steps_here[:, None] + base_pos[None, :]
        queries = jnp.dot(flat_rows, proj_query, preferred_element_type=jnp.float32)
        queries = rotate(
            queries.reshape(block_steps, total_reqs, kv_local, group_size, HD), positions
        ).astype(jnp.bfloat16)
        key_new = jnp.dot(flat_rows, proj_key, preferred_element_type=jnp.float32)
        key_new = rotate(key_new.reshape(block_steps, total_reqs, kv_local, HD), positions).astype(
            jnp.bfloat16
        )
        value_new = jnp.dot(flat_rows, proj_value, preferred_element_type=jnp.float32)
        value_new = value_new.reshape(block_steps, total_reqs, kv_local, HD).astype(jnp.bfloat16)
        every_key = jnp.concatenate(prior_keys + [key_new], axis=0).transpose(0, 2, 1, 3)
        every_value = jnp.concatenate(prior_values + [value_new], axis=0).transpose(0, 2, 1, 3)
        token_ids = jnp.arange(every_key.shape[0], dtype=jnp.int32)
        fresh_valid = jnp.broadcast_to(
            token_ids[None, None, :] <= steps_here[:, None, None],
            (block_steps, total_reqs, every_key.shape[0]),
        )
        long_valid = long_age[None, :, :] > steps_here[:, None, None]
        short_valid = short_live[None]
        long_part = partial_softmax(queries[:, :LONG], long_key_view, long_value_view, long_valid)
        short_part = partial_softmax(
            queries[:, LONG:], short_key_view, short_value_view, short_valid
        )
        old_top = jnp.concatenate([long_part[0], short_part[0]], axis=1)
        old_sum = jnp.concatenate([long_part[1], short_part[1]], axis=1)
        old_acc = jnp.concatenate([long_part[2], short_part[2]], axis=1)
        global_top = lax.pmax(old_top, "seq")
        rescale = jnp.exp(old_top - global_top)
        old_sum, old_acc = lax.psum((old_sum * rescale, old_acc * rescale[..., None]), "seq")
        old_top = global_top
        new_top, new_sum, new_acc = partial_softmax(queries, every_key, every_value, fresh_valid)
        both_top = jnp.maximum(old_top, new_top)
        old_factor = jnp.exp(old_top - both_top)
        new_factor = jnp.exp(new_top - both_top)
        attended = (old_acc * old_factor[..., None] + new_acc * new_factor[..., None]) / (
            old_sum * old_factor + new_sum * new_factor
        )[..., None]
        attended = attended.astype(jnp.bfloat16).reshape(
            block_steps * total_reqs, kv_local * group_size * HD
        )
        head_term = jnp.dot(attended, proj_out, preferred_element_type=jnp.float32).reshape(
            block_steps, total_reqs, model_width
        )
        stream_full = full_rows.astype(jnp.float32) + lax.psum(
            head_term.astype(jnp.bfloat16), "tp"
        ).astype(jnp.float32)
        mlp_in = rms_scaled(stream_full, mlp_gain).astype(jnp.bfloat16)
        stream = lax.dynamic_slice_in_dim(
            stream_full, tp_rank * local_width, local_width, stream_full.ndim - 1
        )
        mlp_flat = mlp_in.reshape(block_steps * total_reqs, model_width)
        gate_act = jnp.dot(mlp_flat, proj_gate, preferred_element_type=jnp.float32)
        up_act = jnp.dot(mlp_flat, proj_up, preferred_element_type=jnp.float32)
        hidden_act = (jax.nn.silu(gate_act) * up_act).astype(jnp.bfloat16)
        down_term = jnp.dot(hidden_act, proj_down, preferred_element_type=jnp.float32).reshape(
            block_steps, total_reqs, model_width
        )
        result = (
            stream
            + lax.psum_scatter(
                down_term.astype(jnp.bfloat16), "tp", scatter_dimension=2, tiled=True
            ).astype(jnp.float32)
        ).astype(jnp.bfloat16)
        result, key_new, value_new = (result, key_new, value_new)
        collected.append(result)
        prior_keys = prior_keys + [key_new]
        prior_values = prior_values + [value_new]
    output = jnp.concatenate(collected, axis=0)
    return output


def solution(mesh):
    in_specs = (
        P(None, None, "tp"),
        P(),
        P(),
        P(None, "tp"),
        P(None, "tp"),
        P(None, "tp"),
        P("tp", None),
        P(None, "tp"),
        P(None, "tp"),
        P("tp", None),
        P("seq", "tp", None),
        P("seq", "tp", None),
        P("seq", "tp", None),
        P("seq", "tp", None),
        P(),
        P(),
    )
    out_specs = P(None, None, "tp")
    return jax.shard_map(body, mesh=mesh, in_specs=in_specs, out_specs=out_specs, check_vma=False)
```

profile of v0, /device:TPU:2, one launch (start us, length us, event | category | flops | bytes accessed | tf_op | source)
XLA Modules:
  0.0 888.0 jit_solution(83622997668964139)
XLA Ops:
  9.4 14.6 %all_gather.24 = bf16[1,4,2560]{1,0,2:T(2,128)(2,1)S(1)} all-gather(bf16[1,4,320]{1,0,2:T(2,128)(2,1)} %copy.291), channel_id=1, replica_groups=mesh['seq'=32,'tp'=8] {'tp'}, dimensions={2}, use_global_device_ids=true | all-gather | bytes 23040 | tf_op jit(solution)/shard_map/all_gather | solution.py:105
  26.6 14.5 %all_gather.25 = bf16[1,4,2560]{1,0,2:T(2,128)(2,1)S(1)} all-gather(bf16[1,4,320]{1,0,2:T(2,128)(2,1)} %copy.292), channel_id=1, replica_groups=mesh['seq'=32,'tp'=8] {'tp'}, dimensions={2}, use_global_device_ids=true | all-gather | bytes 23040 | tf_op jit(solution)/shard_map/all_gather | solution.py:105
  47.1 2.1 convolution_bitcast_fusion.7
  53.7 15.0 %all_gather.27 = bf16[1,4,2560]{1,0,2:T(2,128)(2,1)S(1)} all-gather(bf16[1,4,320]{1,0,2:T(2,128)(2,1)} %copy.294), channel_id=1, replica_groups=mesh['seq'=32,'tp'=8] {'tp'}, dimensions={2}, use_global_device_ids=true | all-gather | bytes 23040 | tf_op jit(solution)/shard_map/all_gather | solution.py:105
  71.9 2.7 convolution_bitcast_fusion.4
  76.1 15.0 %all_gather.26 = bf16[1,4,2560]{1,0,2:T(2,128)(2,1)S(1)} all-gather(bf16[1,4,320]{1,0,2:T(2,128)(2,1)} %copy.293), channel_id=1, replica_groups=mesh['seq'=32,'tp'=8] {'tp'}, dimensions={2}, use_global_device_ids=true | all-gather | bytes 23040 | tf_op jit(solution)/shard_map/all_gather | solution.py:105
  99.2 15.0 %all_gather.29 = bf16[1,4,2560]{1,0,2:T(2,128)(2,1)S(1)} all-gather(bf16[1,4,320]{1,0,2:T(2,128)(2,1)} %copy.296), channel_id=1, replica_groups=mesh['seq'=32,'tp'=8] {'tp'}, dimensions={2}, use_global_device_ids=true | all-gather | bytes 23040 | tf_op jit(solution)/shard_map/all_gather | solution.py:105
  115.6 2.7 convolution_bitcast_fusion.2
  119.8 15.0 %all_gather.28 = bf16[1,4,2560]{1,0,2:T(2,128)(2,1)S(1)} all-gather(bf16[1,4,320]{1,0,2:T(2,128)(2,1)} %copy.295), channel_id=1, replica_groups=mesh['seq'=32,'tp'=8] {'tp'}, dimensions={2}, use_global_device_ids=true | all-gather | bytes 23040 | tf_op jit(solution)/shard_map/all_gather | solution.py:105
  144.6 15.0 %all_gather.31 = bf16[1,4,2560]{1,0,2:T(2,128)(2,1)S(1)} all-gather(bf16[1,4,320]{1,0,2:T(2,128)(2,1)} %copy.298), channel_id=1, replica_groups=mesh['seq'=32,'tp'=8] {'tp'}, dimensions={2}, use_global_device_ids=true | all-gather | bytes 23040 | tf_op jit(solution)/shard_map/all_gather | solution.py:105
  161.0 2.7 convolution_bitcast_fusion
  165.2 15.3 %all_gather.30 = bf16[1,4,2560]{1,0,2:T(2,128)(2,1)S(1)} all-gather(bf16[1,4,320]{1,0,2:T(2,128)(2,1)} %copy.297), channel_id=1, replica_groups=mesh['seq'=32,'tp'=8] {'tp'}, dimensions={2}, use_global_device_ids=true | all-gather | bytes 23040 | tf_op jit(solution)/shard_map/all_gather | solution.py:105
  183.3 2.1 convolution_bitcast_fusion.1
  204.0 140.7 %all-reduce.1 = (f32[1,4,1,4]{3,1,2,0:T(4,128)S(1)}, f32[1,4,1,4]{3,1,2,0:T(4,128)S(1)}, f32[1,4,1,4]{3,1,2,0:T(4,128)S(1)}, f32[1,4,1,4]{3,1,2,0:T(4,128)S(1)},...) all-reduce(f32[1,4,1,4]{3,1,2,0:T(4,128)S(1)} %pad_maximum_fusion.1, ...), channel_id=1, replica_groups=mesh['seq'=32,'tp'=8] {'seq'}, use_global_device_ids=true, to_apply=%region_3.4 | all-reduce | flops 128 | bytes 1024 | tf_op jit(solution)/shard_map/pmax | solution.py:136
  345.4 140.2 %all-reduce = (f32[1,4,1,4,80]{4,3,1,0,2:T(4,128)S(1)}, f32[1,4,1,4]{3,1,2,0:T(4,128)S(1)}, f32[1,4,1,4,80]{4,3,1,0,2:T(4,128)S(1)}, f32[1,4,1,4]{3,1,2,0:T(4,12...) all-reduce(f32[1,4,1,4,80]{4,3,1,0,2:T(4,128)S(1)} %maximum_multipl, ...), channel_id=1, replica_groups=mesh['seq'=32,'tp'=8] {'seq'}, use_global_device_ids=true, to_apply=%region_4.5 | all-reduce | flops 10368 | bytes 82944 | tf_op jit(solution)/shard_map/psum | solution.py:138
  489.1 2.4 fusion
  491.5 2.4 fusion.2
  495.1 2.4 fusion.4
  498.6 2.4 fusion.6
  502.3 2.4 fusion.8
  506.0 2.4 fusion.10
  509.4 2.4 fusion.12
  512.9 2.4 fusion.14
  515.4 62.3 %all-reduce.5.cloned.1.call-done = (bf16[1,4,2560]{2,1,0:T(4,128)(2,1)}, bf16[1,4,2560]{2,1,0:T(4,128)(2,1)}, bf16[1,4,2560]{2,1,0:T(4,128)(2,1)}, bf16[1,4,2560...) async-done(((bf16[1,4,2560]{2,1,0:T(4,128)(2,1)}, ...) | async-done | bytes 163856 | tf_op jit(solution)/shard_map/psum | solution.py:153
  579.2 2.3 fusion.633
  581.5 3.5 fusion.1
  585.1 2.1 copy.259
  589.9 2.3 fusion.629
  592.3 3.5 fusion.3
  596.5 2.3 fusion.625
  598.8 3.6 fusion.5
  603.2 2.3 fusion.621
  605.5 3.6 fusion.7
  609.8 2.3 fusion.617
  612.1 3.5 fusion.9
  616.4 2.3 fusion.613
  618.7 3.6 fusion.11
  626.7 2.9 fusion.609
  632.8 3.5 fusion.13
  636.3 2.1 copy.265
  648.8 3.0 fusion.605
  654.9 3.5 fusion.15
  663.5 32.1 %reduce-scatter.29.cloned.1.call-done = bf16[320,4]{1,0:T(8,128)(2,1)} async-done(((bf16[2560,4]{1,0:T(8,128)(2,1)}), bf16[320,4]{1,0:T(8,128)(2,1)}) %reduce-scatter.29.cloned.1.call-update) | async-done | bytes 2576
  696.6 34.4 %reduce-scatter.31.cloned.1.call-done = bf16[320,4]{1,0:T(8,128)(2,1)} async-done(((bf16[2560,4]{1,0:T(8,128)(2,1)}), bf16[320,4]{1,0:T(8,128)(2,1)}) %reduce-scatter.31.cloned.1.call-update) | async-done | bytes 2576
  732.0 34.4 %reduce-scatter.33.cloned.1.call-done = bf16[320,4]{1,0:T(8,128)(2,1)} async-done(((bf16[2560,4]{1,0:T(8,128)(2,1)}), bf16[320,4]{1,0:T(8,128)(2,1)}) %reduce-scatter.33.cloned.1.call-update) | async-done | bytes 2576
  767.4 34.6 %reduce-scatter.35.cloned.1.call-done = bf16[320,4]{1,0:T(8,128)(2,1)} async-done(((bf16[2560,4]{1,0:T(8,128)(2,1)}), bf16[320,4]{1,0:T(8,128)(2,1)}) %reduce-scatter.35.cloned.1.call-update) | async-done | bytes 2576
  802.9 34.6 %reduce-scatter.37.cloned.1.call-done = bf16[320,4]{1,0:T(8,128)(2,1)} async-done(((bf16[2560,4]{1,0:T(8,128)(2,1)}), bf16[320,4]{1,0:T(8,128)(2,1)}) %reduce-scatter.37.cloned.1.call-update) | async-done | bytes 2576
  839.2 33.8 %reduce-scatter.39.cloned.1.call-done = bf16[320,4]{1,0:T(8,128)(2,1)} async-done(((bf16[2560,4]{1,0:T(8,128)(2,1)}), bf16[320,4]{1,0:T(8,128)(2,1)}) %reduce-scatter.39.cloned.1.call-update) | async-done | bytes 2576
  (506 shorter events, 122.7 us)
Async XLA Ops:
  6.5 575.0 %copy-start = (bf16[432,2560]{1,0:T(8,128)(2,1)S(1)}, bf16[432,2560]{1,0:T(8,128)(2,1)}, u32[]{:S(2)}) copy-start(bf16[432,2560]{1,0:T(8,128)(2,1)} %param.25) | copy-start | bytes 6635524
  6.5 571.1 %all-reduce.5.cloned.1.call-start = ((), (), s32[]{:S(2)}) async-start(), calls=%async_computation.16 | async-start | bytes 327680 | tf_op jit(solution)/shard_map/psum | solution.py:153
  41.8 27.0 %copy-start.2 = (bf16[1,4,2560]{2,1,0:T(4,128)(2,1)}, bf16[1,4,2560]{2,1,0:T(4,128)(2,1)S(1)}, u32[]{:S(2)}) copy-start(bf16[1,4,2560]{2,1,0:T(4,128)(2,1)S(1)} %copy.174) | copy-start | bytes 61444
  41.8 11.1 %copy-start.52 = (bf16[1,4,320]{2,1,0:T(4,128)(2,1)S(1)}, bf16[1,4,320]{2,1,0:T(4,128)(2,1)}, u32[]{:S(2)}) copy-start(bf16[1,4,320]{2,1,0:T(4,128)(2,1)} %get-tuple-element.79) | copy-start | bytes 7684
  44.0 8.8 copy-start.62
  44.1 8.8 copy-start.58
  44.1 8.8 copy-start.60
  44.1 8.8 copy-start.64
  44.1 8.8 copy-start.66
  44.1 8.8 copy-start.68
  114.9 21.6 %copy-start.11 = (bf16[1,4,2560]{2,1,0:T(4,128)(2,1)}, bf16[1,4,2560]{2,1,0:T(4,128)(2,1)S(1)}, u32[]{:S(2)}) copy-start(bf16[1,4,2560]{2,1,0:T(4,128)(2,1)S(1)} %copy.223) | copy-start | bytes 61444
  165.2 21.5 %copy-start.1 = (bf16[128,1,80]{0,2,1:T(8,128)(2,1)S(1)}, bf16[128,1,80]{0,2,1:T(8,128)(2,1)}, u32[]{:S(2)}) copy-start(bf16[128,1,80]{0,2,1:T(8,128)(2,1)} %param.26) | copy-start | bytes 61444
  182.2 12.5 %copy-start.75 = (bf16[1,1,1,4,80]{4,1,3,2,0:T(2,128)(2,1)S(1)}, bf16[1,1,1,4,80]{4,1,3,2,0:T(2,128)(2,1)}, u32[]{:S(2)}) copy-start(bf16[1,1,1,4,80]{4,1,3,2,0:T(2,128)(2,1)} %fusion.448) | copy-start | bytes 1924
  182.2 12.8 %copy-start.100 = (bf16[128,1,80]{0,2,1:T(8,128)(2,1)S(1)}, bf16[128,1,80]{0,2,1:T(8,128)(2,1)}, u32[]{:S(2)}) copy-start(bf16[128,1,80]{0,2,1:T(8,128)(2,1)} %param.27) | copy-start | bytes 61444
  182.2 13.2 %copy-start.74 = (bf16[1,1,1,4,80]{4,1,3,2,0:T(2,128)(2,1)S(1)}, bf16[1,1,1,4,80]{4,1,3,2,0:T(2,128)(2,1)}, u32[]{:S(2)}) copy-start(bf16[1,1,1,4,80]{4,1,3,2,0:T(2,128)(2,1)} %fusion.447) | copy-start | bytes 1924
  182.2 14.4 %copy-start.55 = (bf16[16,1,240]{2,0,1:T(8,128)(2,1)S(1)}, bf16[16,1,240]{2,0,1:T(8,128)(2,1)}, u32[]{:S(2)}) copy-start(bf16[16,1,240]{2,0,1:T(8,128)(2,1)} %param.29) | copy-start | bytes 23044
  182.3 14.5 %copy-start.56 = (bf16[16,1,240]{2,0,1:T(8,128)(2,1)S(1)}, bf16[16,1,240]{2,0,1:T(8,128)(2,1)}, u32[]{:S(2)}) copy-start(bf16[16,1,240]{2,0,1:T(8,128)(2,1)} %param.28) | copy-start | bytes 23044
  182.3 14.6 %copy-start.96 = (s32[3]{0:T(128)S(1)}, s32[3]{0:T(128)}, u32[]{:S(2)}) copy-start(s32[3]{0:T(128)} %param.31) | copy-start | bytes 40
  182.3 14.7 %copy-start.76 = (bf16[3,4,80]{2,0,1:T(4,128)(2,1)S(1)}, bf16[3,4,80]{2,0,1:T(4,128)(2,1)}, u32[]{:S(2)}) copy-start(bf16[3,4,80]{2,0,1:T(4,128)(2,1)} %fusion.260) | copy-start | bytes 5764
  182.3 15.1 %copy-start.77 = (bf16[3,4,80]{2,0,1:T(4,128)(2,1)S(1)}, bf16[3,4,80]{2,0,1:T(4,128)(2,1)}, u32[]{:S(2)}) copy-start(bf16[3,4,80]{2,0,1:T(4,128)(2,1)} %fusion.259) | copy-start | bytes 5764
  182.3 15.3 %copy-start.79 = (bf16[3,4,80]{2,0,1:T(4,128)(2,1)S(1)}, bf16[3,4,80]{2,0,1:T(4,128)(2,1)}, u32[]{:S(2)}) copy-start(bf16[3,4,80]{2,0,1:T(4,128)(2,1)} %fusion.258) | copy-start | bytes 5764
  182.3 15.5 %copy-start.78 = (bf16[3,4,80]{2,0,1:T(4,128)(2,1)S(1)}, bf16[3,4,80]{2,0,1:T(4,128)(2,1)}, u32[]{:S(2)}) copy-start(bf16[3,4,80]{2,0,1:T(4,128)(2,1)} %fusion.257) | copy-start | bytes 5764
  182.3 15.7 %copy-start.81 = (bf16[3,4,80]{2,0,1:T(4,128)(2,1)S(1)}, bf16[3,4,80]{2,0,1:T(4,128)(2,1)}, u32[]{:S(2)}) copy-start(bf16[3,4,80]{2,0,1:T(4,128)(2,1)} %fusion.256) | copy-start | bytes 5764
  182.3 15.9 %copy-start.80 = (bf16[3,4,80]{2,0,1:T(4,128)(2,1)S(1)}, bf16[3,4,80]{2,0,1:T(4,128)(2,1)}, u32[]{:S(2)}) copy-start(bf16[3,4,80]{2,0,1:T(4,128)(2,1)} %fusion.255) | copy-start | bytes 5764
  182.3 18.7 %copy-start.3 = (bf16[1,4,2560]{2,1,0:T(4,128)(2,1)S(1)}, bf16[1,4,2560]{2,1,0:T(4,128)(2,1)}, u32[]{:S(2)}) copy-start(bf16[1,4,2560]{2,1,0:T(4,128)(2,1)} %copy-done.2) | copy-start | bytes 61444
  182.3 18.7 %copy-start.91 = (f32[4]{0:T(128)S(1)}, f32[4]{0:T(128)}, u32[]{:S(2)}) copy-start(f32[4]{0:T(128)} %copy-done.90) | copy-start | bytes 52
  182.4 18.7 %copy-start.98 = (bf16[2560,80]{0,1:T(8,128)(2,1)S(1)}, bf16[2560,80]{0,1:T(8,128)(2,1)}, u32[]{:S(2)}) copy-start(bf16[2560,80]{0,1:T(8,128)(2,1)} %param.20) | copy-start | bytes 1228804
  182.4 19.0 %copy-start.8 = (bf16[1,4,2560]{2,1,0:T(4,128)(2,1)S(1)}, bf16[1,4,2560]{2,1,0:T(4,128)(2,1)}, u32[]{:S(2)}) copy-start(bf16[1,4,2560]{2,1,0:T(4,128)(2,1)} %copy.166) | copy-start | bytes 61444
  182.4 19.0 %copy-start.95 = (f32[4]{0:T(128)S(1)}, f32[4]{0:T(128)}, u32[]{:S(2)}) copy-start(f32[4]{0:T(128)} %copy-done.94) | copy-start | bytes 52
  183.3 18.3 %copy-start.19 = (bf16[1,4,2560]{2,1,0:T(4,128)(2,1)S(1)}, bf16[1,4,2560]{2,1,0:T(4,128)(2,1)}, u32[]{:S(2)}) copy-start(bf16[1,4,2560]{2,1,0:T(4,128)(2,1)} %copy.212) | copy-start | bytes 61444
  183.3 18.3 %copy-start.87 = (f32[4]{0:T(128)S(1)}, f32[4]{0:T(128)}, u32[]{:S(2)}) copy-start(f32[4]{0:T(128)} %copy-done.86) | copy-start | bytes 52
  183.3 18.6 %copy-start.9 = (bf16[1,4,2560]{2,1,0:T(4,128)(2,1)S(1)}, bf16[1,4,2560]{2,1,0:T(4,128)(2,1)}, u32[]{:S(2)}) copy-start(bf16[1,4,2560]{2,1,0:T(4,128)(2,1)} %copy.200) | copy-start | bytes 61444
  183.3 18.6 %copy-start.89 = (f32[4]{0:T(128)S(1)}, f32[4]{0:T(128)}, u32[]{:S(2)}) copy-start(f32[4]{0:T(128)} %copy-done.88) | copy-start | bytes 52
  185.5 16.7 %copy-start.15 = (bf16[1,4,2560]{2,1,0:T(4,128)(2,1)S(1)}, bf16[1,4,2560]{2,1,0:T(4,128)(2,1)}, u32[]{:S(2)}) copy-start(bf16[1,4,2560]{2,1,0:T(4,128)(2,1)} %copy-done.14) | copy-start | bytes 61444
  185.5 16.7 %copy-start.93 = (f32[4]{0:T(128)S(1)}, f32[4]{0:T(128)}, u32[]{:S(2)}) copy-start(f32[4]{0:T(128)} %copy-done.92) | copy-start | bytes 52
  185.5 17.0 %copy-start.6 = (bf16[1,4,2560]{2,1,0:T(4,128)(2,1)S(1)}, bf16[1,4,2560]{2,1,0:T(4,128)(2,1)}, u32[]{:S(2)}) copy-start(bf16[1,4,2560]{2,1,0:T(4,128)(2,1)} %copy-done.5) | copy-start | bytes 61444
  185.5 17.0 %copy-start.83 = (f32[4]{0:T(128)S(1)}, f32[4]{0:T(128)}, u32[]{:S(2)}) copy-start(f32[4]{0:T(128)} %copy-done.82) | copy-start | bytes 52
  187.8 15.0 %copy-start.17 = (bf16[1,4,2560]{2,1,0:T(4,128)(2,1)S(1)}, bf16[1,4,2560]{2,1,0:T(4,128)(2,1)}, u32[]{:S(2)}) copy-start(bf16[1,4,2560]{2,1,0:T(4,128)(2,1)} %copy.234) | copy-start | bytes 61444
  201.3 285.8 %copy-start.41 = (bf16[1,4,1,4,40]{4,1,3,2,0:T(4,128)(2,1)S(1)}, bf16[1,4,1,4,40]{4,1,3,2,0:T(4,128)(2,1)}, u32[]{:S(2)}) copy-start(bf16[1,4,1,4,40]{4,1,3,2,0:T(4,128)(2,1)} %copy-done.40) | copy-start | bytes 3844
  201.4 285.7 %copy-start.43 = (bf16[1,4,1,4,40]{4,1,3,2,0:T(4,128)(2,1)S(1)}, bf16[1,4,1,4,40]{4,1,3,2,0:T(4,128)(2,1)}, u32[]{:S(2)}) copy-start(bf16[1,4,1,4,40]{4,1,3,2,0:T(4,128)(2,1)} %copy-done.42) | copy-start | bytes 3844
  515.3 146.2 %reduce-scatter.25.cloned.1.call-start = ((), (), s32[]{:S(2)}) async-start(), calls=%async_computation.8 | async-start | bytes 737280
  588.2 74.4 %reduce-scatter.27.cloned.1.call-start = ((), (), s32[]{:S(2)}) async-start(), calls=%async_computation.9 | async-start | bytes 737280
  626.6 69.0 %reduce-scatter.29.cloned.1.call-start = ((), (), s32[]{:S(2)}) async-start(), calls=%async_computation.10 | async-start | bytes 737280
  632.7 98.3 %reduce-scatter.31.cloned.1.call-start = ((), (), s32[]{:S(2)}) async-start(), calls=%async_computation.11 | async-start | bytes 737280
  639.4 127.0 %reduce-scatter.33.cloned.1.call-start = ((), (), s32[]{:S(2)}) async-start(), calls=%async_computation.12 | async-start | bytes 737280
  644.5 157.4 %reduce-scatter.35.cloned.1.call-start = ((), (), s32[]{:S(2)}) async-start(), calls=%async_computation.13 | async-start | bytes 737280
  648.7 188.7 %reduce-scatter.37.cloned.1.call-start = ((), (), s32[]{:S(2)}) async-start(), calls=%async_computation.14 | async-start | bytes 737280
  654.8 218.2 %reduce-scatter.39.cloned.1.call-start = ((), (), s32[]{:S(2)}) async-start(), calls=%async_computation.15 | async-start | bytes 737280
  (62 other events, 286.9 us)
Sparse Core Ops, SparseCore 0:
  515.4 62.2 all-reduce.4
  588.3 33.4 reduce-scatter.24
  626.7 33.4 reduce-scatter.26
  662.6 32.9 reduce-scatter.28
  698.0 32.9 reduce-scatter.30
  733.4 32.9 reduce-scatter.32
  768.9 32.9 reduce-scatter.34
  804.5 32.9 reduce-scatter.36
  840.0 32.9 reduce-scatter.38
where the time goes:
time: 892 us; the launch traced here: 888 us
  blocking collectives  400 us (45%)
  waiting for transfers between devices  266 us (30%)
  matrix products  107 us (12%)
  local copies, waits for them, and re-layouts  57.8 us (6%)
  other arithmetic  41 us (5%)
  between operations  15.4 us (2%)
    unnamed x17, waiting for transfers between devices  204 us
    pmax x1, blocking collectives, body(): global_top = lax.pmax(old_top, 'seq')  141 us
    psum x1, blocking collectives, body(): lax.psum((old_sum * rescale, old_acc * rescale[..., None]), 'seq')  140 us
    all_gather x8, blocking collectives, body(): full_rows = lax.all_gather(token_rows, 'tp', axis=2, tiled=True)  120 us
    psum x1, waiting for transfers between devices, body(): lax.psum(head_term.astype(jnp.bfloat16), 'tp').astype(jnp.float32)  62.3 us
    unnamed x247, local copies, waits for them, and re-layouts  45.7 us
    dot_general x8, matrix products, body(): jnp.dot(hidden_act, proj_down, preferred_element_type=jnp.float32)  28.3 us
    dot_general x8, matrix products, body(): gate_act = jnp.dot(mlp_flat, proj_gate, preferred_element_type=jnp.float32)  19.7 us
  transfers between devices with their start and end apart: 9, of which 7 were waited for; matrix products, arithmetic and copies ran while one was open for 9% of the time, Pallas kernels for 0%

commit v1 on v0

--- a/solution.py
+++ b/solution.py
@@ -150,8 +150,8 @@
         head_term = jnp.dot(attended, proj_out, preferred_element_type=jnp.float32).reshape(
             block_steps, total_reqs, model_width
         )
-        stream_full = full_rows.astype(jnp.float32) + lax.psum(
-            head_term.astype(jnp.bfloat16), "tp"
+        stream_full = full_rows.astype(jnp.float32) + jnp.sum(
+            lax.all_gather(head_term.astype(jnp.bfloat16), "tp"), axis=0
         ).astype(jnp.float32)
         mlp_in = rms_scaled(stream_full, mlp_gain).astype(jnp.bfloat16)
         stream = lax.dynamic_slice_in_dim(

time: 892 us -> 811 us (0.909)
  waiting for transfers between devices: 266 us -> 51.1 us
  blocking collectives: 400 us -> 504 us
  matrix products: 107 us -> 122 us
  other arithmetic: 41 us -> 54.4 us
    unnamed x17 -> x16, waiting for transfers between devices: 204 us -> 51.1 us
    all_gather x0 -> x8, blocking collectives: none -> 103 us  [body(): lax.all_gather(head_term.astype(jnp.bfloat16), 'tp')]
    psum x1 -> x0, waiting for transfers between devices: 62.3 us -> none  [body(): lax.psum(head_term.astype(jnp.bfloat16), 'tp').astype(jnp.float32)]
    dot_general x8, matrix products: 4.09 us -> 14.1 us  [body(): jnp.dot(flat_rows, proj_value, preferred_element_type=jnp.float32)]
    unnamed x247 -> x265, local copies, waits for them, and re-layouts: 45.7 us -> 47 us
  transfers between devices with their start and end apart: 9 -> 8, of which waited for: 7 -> 2; matrix products, arithmetic and copies ran while one was open for 9% -> 17% of each run, Pallas kernels for 0% -> 0%
where the time goes in v1:
time: 811 us; the launch traced here: 807 us
  blocking collectives  504 us (62%)
  matrix products  122 us (15%)
  local copies, waits for them, and re-layouts  59 us (7%)
  other arithmetic  54.4 us (7%)
  waiting for transfers between devices  51.1 us (6%)
  between operations  15.7 us (2%)
    pmax x1, blocking collectives, body(): global_top = lax.pmax(old_top, 'seq')  141 us
    psum x1, blocking collectives, body(): lax.psum((old_sum * rescale, old_acc * rescale[..., None]), 'seq')  141 us
    all_gather x8, blocking collectives, body(): full_rows = lax.all_gather(token_rows, 'tp', axis=2, tiled=True)  119 us
    all_gather x8, blocking collectives, body(): lax.all_gather(head_term.astype(jnp.bfloat16), 'tp')  103 us
    unnamed x16, waiting for transfers between devices  51.1 us
    unnamed x265, local copies, waits for them, and re-layouts  47 us
    dot_general x8, matrix products, body(): jnp.dot(hidden_act, proj_down, preferred_element_type=jnp.float32)  27.8 us
    dot_general x8, matrix products, body(): queries = jnp.dot(flat_rows, proj_query, preferred_element_type=jnp.float32)  18.7 us
  transfers between devices with their start and end apart: 8, of which 2 were waited for; matrix products, arithmetic and copies ran while one was open for 17% of the time, Pallas kernels for 0%

profile of v1, /device:TPU:2, one launch (start us, length us, event | category | flops | bytes accessed | tf_op | source)
XLA Modules:
  0.0 806.8 jit_solution(13618688698330139441)
XLA Ops:
  9.4 14.6 %all_gather.72 = bf16[1,4,2560]{1,0,2:T(2,128)(2,1)S(1)} all-gather(bf16[1,4,320]{1,0,2:T(2,128)(2,1)} %copy.596), channel_id=1, replica_groups=mesh['seq'=32,'tp'=8] {'tp'}, dimensions={2}, use_global_device_ids=true | all-gather | bytes 23040 | tf_op jit(solution)/shard_map/all_gather | solution.py:105
  26.6 14.5 %all_gather.75 = bf16[1,4,2560]{1,0,2:T(2,128)(2,1)S(1)} all-gather(bf16[1,4,320]{1,0,2:T(2,128)(2,1)} %copy.597), channel_id=1, replica_groups=mesh['seq'=32,'tp'=8] {'tp'}, dimensions={2}, use_global_device_ids=true | all-gather | bytes 23040 | tf_op jit(solution)/shard_map/all_gather | solution.py:105
  47.1 2.1 convolution_bitcast_fusion.7
  53.8 15.0 %all_gather.81 = bf16[1,4,2560]{1,0,2:T(2,128)(2,1)S(1)} all-gather(bf16[1,4,320]{1,0,2:T(2,128)(2,1)} %copy.599), channel_id=1, replica_groups=mesh['seq'=32,'tp'=8] {'tp'}, dimensions={2}, use_global_device_ids=true | all-gather | bytes 23040 | tf_op jit(solution)/shard_map/all_gather | solution.py:105
  70.2 2.7 convolution_bitcast_fusion.4
  74.4 15.0 %all_gather.78 = bf16[1,4,2560]{1,0,2:T(2,128)(2,1)S(1)} all-gather(bf16[1,4,320]{1,0,2:T(2,128)(2,1)} %copy.598), channel_id=1, replica_groups=mesh['seq'=32,'tp'=8] {'tp'}, dimensions={2}, use_global_device_ids=true | all-gather | bytes 23040 | tf_op jit(solution)/shard_map/all_gather | solution.py:105
  99.2 15.0 %all_gather.87 = bf16[1,4,2560]{1,0,2:T(2,128)(2,1)S(1)} all-gather(bf16[1,4,320]{1,0,2:T(2,128)(2,1)} %copy.601), channel_id=1, replica_groups=mesh['seq'=32,'tp'=8] {'tp'}, dimensions={2}, use_global_device_ids=true | all-gather | bytes 23040 | tf_op jit(solution)/shard_map/all_gather | solution.py:105
  115.6 2.7 convolution_bitcast_fusion.2
  119.8 15.0 %all_gather.84 = bf16[1,4,2560]{1,0,2:T(2,128)(2,1)S(1)} all-gather(bf16[1,4,320]{1,0,2:T(2,128)(2,1)} %copy.600), channel_id=1, replica_groups=mesh['seq'=32,'tp'=8] {'tp'}, dimensions={2}, use_global_device_ids=true | all-gather | bytes 23040 | tf_op jit(solution)/shard_map/all_gather | solution.py:105
  144.6 15.0 %all_gather.93 = bf16[1,4,2560]{1,0,2:T(2,128)(2,1)S(1)} all-gather(bf16[1,4,320]{1,0,2:T(2,128)(2,1)} %copy.603), channel_id=1, replica_groups=mesh['seq'=32,'tp'=8] {'tp'}, dimensions={2}, use_global_device_ids=true | all-gather | bytes 23040 | tf_op jit(solution)/shard_map/all_gather | solution.py:105
  161.1 2.7 convolution_bitcast_fusion
  165.3 15.1 %all_gather.90 = bf16[1,4,2560]{1,0,2:T(2,128)(2,1)S(1)} all-gather(bf16[1,4,320]{1,0,2:T(2,128)(2,1)} %copy.602), channel_id=1, replica_groups=mesh['seq'=32,'tp'=8] {'tp'}, dimensions={2}, use_global_device_ids=true | all-gather | bytes 23040 | tf_op jit(solution)/shard_map/all_gather | solution.py:105
  183.3 2.2 convolution_bitcast_fusion.1
  202.8 140.9 %all-reduce.1 = (f32[1,4,1,4]{3,1,2,0:T(4,128)S(1)}, f32[1,4,1,4]{3,1,2,0:T(4,128)S(1)}, f32[1,4,1,4]{3,1,2,0:T(4,128)S(1)}, f32[1,4,1,4]{3,1,2,0:T(4,128)S(1)},...) all-reduce(f32[1,4,1,4]{3,1,2,0:T(4,128)S(1)} %pad_maximum_fusion.1, ...), channel_id=1, replica_groups=mesh['seq'=32,'tp'=8] {'seq'}, use_global_device_ids=true, to_apply=%region_3.4 | all-reduce | flops 128 | bytes 1024 | tf_op jit(solution)/shard_map/pmax | solution.py:136
  344.6 140.8 %all-reduce = (f32[1,4,1,4,80]{4,3,1,0,2:T(4,128)S(1)}, f32[1,4,1,4]{3,1,2,0:T(4,128)S(1)}, f32[1,4,1,4,80]{4,3,1,0,2:T(4,128)}, f32[1,4,1,4]{3,1,2,0:T(4,128)},...) all-reduce(f32[1,4,1,4,80]{4,3,1,0,2:T(4,128)S(1)} %maximum_multipl, ...), channel_id=1, replica_groups=mesh['seq'=32,'tp'=8] {'seq'}, use_global_device_ids=true, to_apply=%region_4.5 | all-reduce | flops 10368 | bytes 82944 | tf_op jit(solution)/shard_map/psum | solution.py:138
  488.3 13.0 %all-gather.8 = bf16[8,4,2560]{2,1,0:T(4,128)(2,1)S(1)} all-gather(bf16[1,4,2560]{2,1,0:T(4,128)(2,1)S(1)} %fusion), channel_id=2, replica_groups=mesh['seq'=32,'tp'=8] {'tp'}, dimensions={0}, use_global_device_ids=true | all-gather | bytes 184320 | tf_op jit(solution)/shard_map/all_gather | solution.py:154
  502.2 2.3 fusion.633
  504.5 3.5 fusion.1
  508.0 2.1 copy.564
  519.6 13.1 %all-gather.9 = bf16[8,4,2560]{2,1,0:T(4,128)(2,1)S(1)} all-gather(bf16[1,4,2560]{2,1,0:T(4,128)(2,1)S(1)} %fusion.2), channel_id=3, replica_groups=mesh['seq'=32,'tp'=8] {'tp'}, dimensions={0}, use_global_device_ids=true | all-gather | bytes 184320 | tf_op jit(solution)/shard_map/all_gather | solution.py:154
  533.5 2.3 fusion.629
  535.8 3.6 fusion.3
  539.4 2.1 copy.566
  553.8 12.8 %all-gather.10 = bf16[8,4,2560]{2,1,0:T(4,128)(2,1)S(1)} all-gather(bf16[1,4,2560]{2,1,0:T(4,128)(2,1)S(1)} %fusion.4), channel_id=4, replica_groups=mesh['seq'=32,'tp'=8] {'tp'}, dimensions={0}, use_global_device_ids=true | all-gather | bytes 184320 | tf_op jit(solution)/shard_map/all_gather | solution.py:154
  567.4 2.3 fusion.625
  569.7 3.5 fusion.5
  573.3 2.1 copy.568
  583.6 12.8 %all-gather.11 = bf16[8,4,2560]{2,1,0:T(4,128)(2,1)S(1)} all-gather(bf16[1,4,2560]{2,1,0:T(4,128)(2,1)S(1)} %fusion.6), channel_id=5, replica_groups=mesh['seq'=32,'tp'=8] {'tp'}, dimensions={0}, use_global_device_ids=true | all-gather | bytes 184320 | tf_op jit(solution)/shard_map/all_gather | solution.py:154
  597.2 2.3 fusion.621
  599.5 3.5 fusion.7
  603.1 2.1 copy.570
  615.9 13.0 %all-gather.12 = bf16[8,4,2560]{2,1,0:T(4,128)(2,1)S(1)} all-gather(bf16[1,4,2560]{2,1,0:T(4,128)(2,1)S(1)} %fusion.8), channel_id=6, replica_groups=mesh['seq'=32,'tp'=8] {'tp'}, dimensions={0}, use_global_device_ids=true | all-gather | bytes 184320 | tf_op jit(solution)/shard_map/all_gather | solution.py:154
  629.7 2.3 fusion.617
  632.0 3.6 fusion.9
  635.6 2.1 copy.572
  651.2 12.8 %all-gather.13 = bf16[8,4,2560]{2,1,0:T(4,128)(2,1)S(1)} all-gather(bf16[1,4,2560]{2,1,0:T(4,128)(2,1)S(1)} %fusion.10), channel_id=7, replica_groups=mesh['seq'=32,'tp'=8] {'tp'}, dimensions={0}, use_global_device_ids=true | all-gather | bytes 184320 | tf_op jit(solution)/shard_map/all_gather | solution.py:154
  664.8 2.3 fusion.613
  667.1 3.6 fusion.11
  670.6 2.1 copy.574
  681.6 12.8 %all-gather.14 = bf16[8,4,2560]{2,1,0:T(4,128)(2,1)S(1)} all-gather(bf16[1,4,2560]{2,1,0:T(4,128)(2,1)S(1)} %fusion.12), channel_id=8, replica_groups=mesh['seq'=32,'tp'=8] {'tp'}, dimensions={0}, use_global_device_ids=true | all-gather | bytes 184320 | tf_op jit(solution)/shard_map/all_gather | solution.py:154
  695.2 2.3 fusion.609
  697.5 3.6 fusion.13
  701.0 2.1 copy.576
  712.0 12.8 %all-gather.15 = bf16[8,4,2560]{2,1,0:T(4,128)(2,1)S(1)} all-gather(bf16[1,4,2560]{2,1,0:T(4,128)(2,1)S(1)} %fusion.14), channel_id=9, replica_groups=mesh['seq'=32,'tp'=8] {'tp'}, dimensions={0}, use_global_device_ids=true | all-gather | bytes 184320 | tf_op jit(solution)/shard_map/all_gather | solution.py:154
  725.6 2.3 fusion.605
  727.9 2.9 fusion.15
  738.8 17.2 %reduce-scatter.37.cloned.1.call-done = bf16[320,4]{1,0:T(8,128)(2,1)} async-done(((bf16[2560,4]{1,0:T(8,128)(2,1)}), bf16[320,4]{1,0:T(8,128)(2,1)}) %reduce-scatter.37.cloned.1.call-update) | async-done | bytes 2576
  757.8 33.7 %reduce-scatter.39.cloned.1.call-done = bf16[320,4]{1,0:T(8,128)(2,1)} async-done(((bf16[2560,4]{1,0:T(8,128)(2,1)}), bf16[320,4]{1,0:T(8,128)(2,1)}) %reduce-scatter.39.cloned.1.call-update) | async-done | bytes 2576
  (537 shorter events, 163.0 us)
Async XLA Ops:
  6.5 497.9 %copy-start = (bf16[432,2560]{1,0:T(8,128)(2,1)S(1)}, bf16[432,2560]{1,0:T(8,128)(2,1)}, u32[]{:S(2)}) copy-start(bf16[432,2560]{1,0:T(8,128)(2,1)} %param.25) | copy-start | bytes 6635524
  6.5 726.3 %reduce-scatter.25.cloned.1.call-start = ((), (), s32[]{:S(2)}) async-start(), calls=%async_computation.8 | async-start | bytes 737280
  69.5 21.6 %copy-start.8 = (bf16[1,4,2560]{2,1,0:T(4,128)(2,1)}, bf16[1,4,2560]{2,1,0:T(4,128)(2,1)S(1)}, u32[]{:S(2)}) copy-start(bf16[1,4,2560]{2,1,0:T(4,128)(2,1)S(1)} %copy.505) | copy-start | bytes 61444
  114.9 21.6 %copy-start.5 = (bf16[1,4,2560]{2,1,0:T(4,128)(2,1)}, bf16[1,4,2560]{2,1,0:T(4,128)(2,1)S(1)}, u32[]{:S(2)}) copy-start(bf16[1,4,2560]{2,1,0:T(4,128)(2,1)S(1)} %copy.528) | copy-start | bytes 61444
  165.3 21.4 %copy-start.1 = (bf16[128,1,80]{0,2,1:T(8,128)(2,1)S(1)}, bf16[128,1,80]{0,2,1:T(8,128)(2,1)}, u32[]{:S(2)}) copy-start(bf16[128,1,80]{0,2,1:T(8,128)(2,1)} %param.26) | copy-start | bytes 61444
  182.2 14.8 %copy-start.80 = (bf16[3,4,80]{2,0,1:T(4,128)(2,1)S(1)}, bf16[3,4,80]{2,0,1:T(4,128)(2,1)}, u32[]{:S(2)}) copy-start(bf16[3,4,80]{2,0,1:T(4,128)(2,1)} %fusion.260) | copy-start | bytes 5764
  182.2 15.2 %copy-start.81 = (bf16[3,4,80]{2,0,1:T(4,128)(2,1)S(1)}, bf16[3,4,80]{2,0,1:T(4,128)(2,1)}, u32[]{:S(2)}) copy-start(bf16[3,4,80]{2,0,1:T(4,128)(2,1)} %fusion.259) | copy-start | bytes 5764
  182.2 15.4 %copy-start.83 = (bf16[3,4,80]{2,0,1:T(4,128)(2,1)S(1)}, bf16[3,4,80]{2,0,1:T(4,128)(2,1)}, u32[]{:S(2)}) copy-start(bf16[3,4,80]{2,0,1:T(4,128)(2,1)} %fusion.258) | copy-start | bytes 5764
  182.2 15.6 %copy-start.82 = (bf16[3,4,80]{2,0,1:T(4,128)(2,1)S(1)}, bf16[3,4,80]{2,0,1:T(4,128)(2,1)}, u32[]{:S(2)}) copy-start(bf16[3,4,80]{2,0,1:T(4,128)(2,1)} %fusion.257) | copy-start | bytes 5764
  182.2 15.8 %copy-start.85 = (bf16[3,4,80]{2,0,1:T(4,128)(2,1)S(1)}, bf16[3,4,80]{2,0,1:T(4,128)(2,1)}, u32[]{:S(2)}) copy-start(bf16[3,4,80]{2,0,1:T(4,128)(2,1)} %fusion.256) | copy-start | bytes 5764
  182.2 16.0 %copy-start.84 = (bf16[3,4,80]{2,0,1:T(4,128)(2,1)S(1)}, bf16[3,4,80]{2,0,1:T(4,128)(2,1)}, u32[]{:S(2)}) copy-start(bf16[3,4,80]{2,0,1:T(4,128)(2,1)} %fusion.255) | copy-start | bytes 5764
  182.2 18.8 %copy-start.12 = (bf16[1,4,2560]{2,1,0:T(4,128)(2,1)S(1)}, bf16[1,4,2560]{2,1,0:T(4,128)(2,1)}, u32[]{:S(2)}) copy-start(bf16[1,4,2560]{2,1,0:T(4,128)(2,1)} %copy-done.11) | copy-start | bytes 61444
  182.2 18.8 %copy-start.94 = (f32[4]{0:T(128)S(1)}, f32[4]{0:T(128)}, u32[]{:S(2)}) copy-start(f32[4]{0:T(128)} %copy-done.93) | copy-start | bytes 52
  182.2 18.8 %copy-start.105 = (bf16[2560,80]{0,1:T(8,128)(2,1)S(1)}, bf16[2560,80]{0,1:T(8,128)(2,1)}, u32[]{:S(2)}) copy-start(bf16[2560,80]{0,1:T(8,128)(2,1)} %param.20) | copy-start | bytes 1228804
  182.3 19.1 %copy-start.14 = (bf16[1,4,2560]{2,1,0:T(4,128)(2,1)S(1)}, bf16[1,4,2560]{2,1,0:T(4,128)(2,1)}, u32[]{:S(2)}) copy-start(bf16[1,4,2560]{2,1,0:T(4,128)(2,1)} %copy.471) | copy-start | bytes 61444
  182.3 19.0 %copy-start.97 = (f32[4]{0:T(128)S(1)}, f32[4]{0:T(128)}, u32[]{:S(2)}) copy-start(f32[4]{0:T(128)} %copy-done.96) | copy-start | bytes 52
  183.2 18.4 %copy-start.44 = (bf16[1,4,1,4,40]{4,1,3,2,0:T(4,128)(2,1)S(1)}, bf16[1,4,1,4,40]{4,1,3,2,0:T(4,128)(2,1)}, u32[]{:S(2)}) copy-start(bf16[1,4,1,4,40]{4,1,3,2,0:T(4,128)(2,1)} %copy-done.43) | copy-start | bytes 3844
  183.2 18.4 %copy-start.46 = (bf16[1,4,1,4,40]{4,1,3,2,0:T(4,128)(2,1)S(1)}, bf16[1,4,1,4,40]{4,1,3,2,0:T(4,128)(2,1)}, u32[]{:S(2)}) copy-start(bf16[1,4,1,4,40]{4,1,3,2,0:T(4,128)(2,1)} %copy-done.45) | copy-start | bytes 3844
  183.2 18.5 %copy-start.56 = (f32[40]{0:T(128)S(1)}, f32[40]{0:T(128)}, u32[]{:S(2)}) copy-start(f32[40]{0:T(128)} %multiply_power_fusion) | copy-start | bytes 484
  183.2 18.5 %copy-start.69 = (f32[4]{0:T(128)S(1)}, f32[4]{0:T(128)}, u32[]{:S(2)}) copy-start(f32[4]{0:T(128)} %copy-done.68) | copy-start | bytes 52
  183.2 18.5 %copy-start.71 = (f32[4]{0:T(128)S(1)}, f32[4]{0:T(128)}, u32[]{:S(2)}) copy-start(f32[4]{0:T(128)} %copy-done.70) | copy-start | bytes 52
  183.3 19.5 %copy-start.67 = (bf16[2560]{0:T(1024)(128)(2,1)S(1)}, bf16[2560]{0:T(1024)(128)(2,1)}, u32[]{:S(2)}) copy-start(bf16[2560]{0:T(1024)(128)(2,1)} %param.18) | copy-start | bytes 15364
  183.3 302.2 %copy-start.106 = (bf16[2560,80]{0,1:T(8,128)(2,1)S(1)}, bf16[2560,80]{0,1:T(8,128)(2,1)}, u32[]{:S(2)}) copy-start(bf16[2560,80]{0,1:T(8,128)(2,1)} %param.21) | copy-start | bytes 1228804
  186.3 300.2 %copy-start.15 = (bf16[1,4,1,4,40]{4,1,3,2,0:T(4,128)(2,1)}, bf16[1,4,1,4,40]{4,1,3,2,0:T(4,128)(2,1)S(1)}, u32[]{:S(2)}) copy-start(bf16[1,4,1,4,40]{4,1,3,2,0:T(4,128)(2,1)S(1)} %get-tuple-element.75) | copy-start | bytes 3844
  186.3 300.2 %copy-start.17 = (bf16[1,4,1,4,40]{4,1,3,2,0:T(4,128)(2,1)}, bf16[1,4,1,4,40]{4,1,3,2,0:T(4,128)(2,1)S(1)}, u32[]{:S(2)}) copy-start(bf16[1,4,1,4,40]{4,1,3,2,0:T(4,128)(2,1)S(1)} %get-tuple-element.76) | copy-start | bytes 3844
  186.3 300.2 %copy-start.19 = (bf16[1,4,1,4,40]{4,1,3,2,0:T(4,128)(2,1)}, bf16[1,4,1,4,40]{4,1,3,2,0:T(4,128)(2,1)S(1)}, u32[]{:S(2)}) copy-start(bf16[1,4,1,4,40]{4,1,3,2,0:T(4,128)(2,1)S(1)} %get-tuple-element.297) | copy-start | bytes 3844
  186.4 300.2 %copy-start.21 = (bf16[1,4,1,4,40]{4,1,3,2,0:T(4,128)(2,1)}, bf16[1,4,1,4,40]{4,1,3,2,0:T(4,128)(2,1)S(1)}, u32[]{:S(2)}) copy-start(bf16[1,4,1,4,40]{4,1,3,2,0:T(4,128)(2,1)S(1)} %get-tuple-element.298) | copy-start | bytes 3844
  202.4 284.1 %copy-start.47 = (bf16[1,4,1,40]{3,1,2,0:T(4,128)(2,1)}, bf16[1,4,1,40]{3,1,2,0:T(4,128)(2,1)S(1)}, u32[]{:S(2)}) copy-start(bf16[1,4,1,40]{3,1,2,0:T(4,128)(2,1)S(1)} %get-tuple-element.218) | copy-start | bytes 964
  202.4 284.1 %copy-start.48 = (bf16[1,4,1,40]{3,1,2,0:T(4,128)(2,1)}, bf16[1,4,1,40]{3,1,2,0:T(4,128)(2,1)S(1)}, u32[]{:S(2)}) copy-start(bf16[1,4,1,40]{3,1,2,0:T(4,128)(2,1)S(1)} %get-tuple-element.219) | copy-start | bytes 964
  343.6 142.9 %copy-start.60 = (f32[1,4,1,4]{3,1,2,0:T(4,128)}, f32[1,4,1,4]{3,1,2,0:T(4,128)S(1)}, u32[]{:S(2)}) copy-start(f32[1,4,1,4]{3,1,2,0:T(4,128)S(1)} %get-tuple-element.35) | copy-start | bytes 196
  343.6 142.9 %copy-start.61 = (f32[1,4,1,4]{3,1,2,0:T(4,128)}, f32[1,4,1,4]{3,1,2,0:T(4,128)S(1)}, u32[]{:S(2)}) copy-start(f32[1,4,1,4]{3,1,2,0:T(4,128)S(1)} %get-tuple-element.34) | copy-start | bytes 196
  343.6 142.9 %copy-start.62 = (f32[1,4,1,4]{3,1,2,0:T(4,128)}, f32[1,4,1,4]{3,1,2,0:T(4,128)S(1)}, u32[]{:S(2)}) copy-start(f32[1,4,1,4]{3,1,2,0:T(4,128)S(1)} %get-tuple-element.33) | copy-start | bytes 196
  343.6 142.9 %copy-start.66 = (f32[1,4,1,4]{3,1,2,0:T(4,128)}, f32[1,4,1,4]{3,1,2,0:T(4,128)S(1)}, u32[]{:S(2)}) copy-start(f32[1,4,1,4]{3,1,2,0:T(4,128)S(1)} %get-tuple-element.30) | copy-start | bytes 196
  343.6 144.7 %copy-start.59 = (f32[1,4,1,4]{3,1,2,0:T(4,128)}, f32[1,4,1,4]{3,1,2,0:T(4,128)S(1)}, u32[]{:S(2)}) copy-start(f32[1,4,1,4]{3,1,2,0:T(4,128)S(1)} %get-tuple-element.36) | copy-start | bytes 196
  511.0 21.7 %copy-start.13 = (bf16[1,4,2560]{2,1,0:T(4,128)(2,1)S(1)}, bf16[1,4,2560]{2,1,0:T(4,128)(2,1)}, u32[]{:S(2)}) copy-start(bf16[1,4,2560]{2,1,0:T(4,128)(2,1)} %copy-done.11) | copy-start | bytes 61444
  511.1 222.8 %reduce-scatter.27.cloned.1.call-start = ((), (), s32[]{:S(2)}) async-start(), calls=%async_computation.9 | async-start | bytes 737280
  542.5 24.1 %copy-start.10 = (bf16[1,4,2560]{2,1,0:T(4,128)(2,1)S(1)}, bf16[1,4,2560]{2,1,0:T(4,128)(2,1)}, u32[]{:S(2)}) copy-start(bf16[1,4,2560]{2,1,0:T(4,128)(2,1)} %copy.492) | copy-start | bytes 61444
  542.5 192.3 %reduce-scatter.29.cloned.1.call-start = ((), (), s32[]{:S(2)}) async-start(), calls=%async_computation.10 | async-start | bytes 737280
  576.3 20.1 %copy-start.9 = (bf16[1,4,2560]{2,1,0:T(4,128)(2,1)S(1)}, bf16[1,4,2560]{2,1,0:T(4,128)(2,1)}, u32[]{:S(2)}) copy-start(bf16[1,4,2560]{2,1,0:T(4,128)(2,1)} %copy-done.8) | copy-start | bytes 61444
  576.4 159.5 %reduce-scatter.31.cloned.1.call-start = ((), (), s32[]{:S(2)}) async-start(), calls=%async_computation.11 | async-start | bytes 737280
  606.1 22.8 %copy-start.7 = (bf16[1,4,2560]{2,1,0:T(4,128)(2,1)S(1)}, bf16[1,4,2560]{2,1,0:T(4,128)(2,1)}, u32[]{:S(2)}) copy-start(bf16[1,4,2560]{2,1,0:T(4,128)(2,1)} %copy.517) | copy-start | bytes 61444
  606.1 130.7 %reduce-scatter.33.cloned.1.call-start = ((), (), s32[]{:S(2)}) async-start(), calls=%async_computation.12 | async-start | bytes 737280
  638.7 25.3 %copy-start.6 = (bf16[1,4,2560]{2,1,0:T(4,128)(2,1)S(1)}, bf16[1,4,2560]{2,1,0:T(4,128)(2,1)}, u32[]{:S(2)}) copy-start(bf16[1,4,2560]{2,1,0:T(4,128)(2,1)} %copy-done.5) | copy-start | bytes 61444
  638.7 99.2 %reduce-scatter.35.cloned.1.call-start = ((), (), s32[]{:S(2)}) async-start(), calls=%async_computation.13 | async-start | bytes 737280
  673.7 20.8 %copy-start.4 = (bf16[1,4,2560]{2,1,0:T(4,128)(2,1)S(1)}, bf16[1,4,2560]{2,1,0:T(4,128)(2,1)}, u32[]{:S(2)}) copy-start(bf16[1,4,2560]{2,1,0:T(4,128)(2,1)} %copy.539) | copy-start | bytes 61444
  673.7 82.3 %reduce-scatter.37.cloned.1.call-start = ((), (), s32[]{:S(2)}) async-start(), calls=%async_computation.14 | async-start | bytes 737280
  704.1 20.7 %copy-start.3 = (bf16[1,4,2560]{2,1,0:T(4,128)(2,1)S(1)}, bf16[1,4,2560]{2,1,0:T(4,128)(2,1)}, u32[]{:S(2)}) copy-start(bf16[1,4,2560]{2,1,0:T(4,128)(2,1)} %copy-done.2) | copy-start | bytes 61444
  704.1 87.3 %reduce-scatter.39.cloned.1.call-start = ((), (), s32[]{:S(2)}) async-start(), calls=%async_computation.15 | async-start | bytes 737280
  (70 other events, 391.9 us)
Sparse Core Ops, SparseCore 0:
  511.2 31.5 reduce-scatter.24
  545.3 32.8 reduce-scatter.26
  580.7 32.8 reduce-scatter.28
  616.0 33.0 reduce-scatter.30
  651.5 33.2 reduce-scatter.32
  687.2 32.9 reduce-scatter.34
  722.7 33.2 reduce-scatter.36
  758.5 32.8 reduce-scatter.38
